TPU v7x, 128 devices: a whole 4x4x4 slice. The times are simulated.
128 devices in a mesh: section: 8 (over y, core), fsdp: 16 (over x, z).
Axes of the slice: x: 4, y: 4, z: 4, core: 2. Of those that a mesh axis runs over, the one named last changes fastest.
Arguments:
- layer_input: bfloat16 [8, 8192, 2048], P('section', 'fsdp'), may hold values from -6 to 6
- resid_grad: bfloat16 [8, 8192, 2048], P('section', 'fsdp'), may hold values from -6 to 6
- qkv_grad: bfloat16 [8, 8192, 3072], P('section', 'fsdp'), may hold values from -6 to 6
- prev_input: bfloat16 [8, 8192, 2048], P('section', 'fsdp'), may hold values from -6 to 6
- prev_qkv_grad: bfloat16 [8, 8192, 3072], P('section', 'fsdp'), may hold values from -0.059814453 to 0.059814453
- qkv_weight: bfloat16 [8, 2048, 3072], P('section', 'fsdp'), may hold values from -0.125 to 0.125
- norm_gain: float32 [8, 2048], P('section'), may hold values from 0.1 to 1.9
Outputs:
- upstream_grad: bfloat16 [8, 8192, 2048], P('section', 'fsdp')
- weight_grad: float32 [8, 2048, 3072], P('section', 'fsdp')
- gain_grad: float32 [8, 2048], P('section')
All inputs are finite; a program needn't handle non-finite values.
Results may differ from a plain program's by a relative error of at most 0.018.
Values may be sent and summed in bfloat16 or wider, within the bound.
A program may use at most 128 MiB of HBM per device.

v0:
```python
import jax
import jax.numpy as jnp
from jax import lax
from jax.sharding import PartitionSpec as P

EPS = 1e-05


def from_behind(block, axis, distance):
    devices = range(lax.axis_size(axis))
    route = [(i - distance, i) for i in devices if i - distance in devices]
    return lax.ppermute(block, axis, route)


def row_scale(rows):
    values = rows.astype(jnp.float32)
    return lax.rsqrt(jnp.mean(values * values, axis=-1, keepdims=True) + EPS)


def transpose_product(grads, piece):
    return lax.dot_general(
        grads, piece, (((1,), (1,)), ((), ())), preferred_element_type=jnp.float32
    )


def local(layer_input, resid_grad, qkv_grad, prev_input, prev_qkv_grad, qkv_weight, norm_gain):
    rows_now = layer_input[0]
    grads_now = qkv_grad[0]
    rows_prev = prev_input[0]
    grads_prev = prev_qkv_grad[0]
    weight_rows = qkv_weight[0]
    gain = norm_gain[0]
    owned = weight_rows.shape[0]
    prev_scale = row_scale(rows_prev)
    prev_normed = (rows_prev.astype(jnp.float32) * prev_scale * gain[None, :]).astype(jnp.bfloat16)
    direction = transpose_product(
        grads_now, lax.all_gather(weight_rows, "fsdp", axis=0, tiled=True)
    )
    scale = row_scale(rows_now)
    values = rows_now.astype(jnp.float32)
    gained = gain[None, :] * direction
    inner = jnp.mean(gained * values, axis=-1, keepdims=True)
    local_grad = (
        resid_grad[0].astype(jnp.float32) + scale * gained - values * scale * scale * scale * inner
    ).astype(jnp.bfloat16)
    upstream_grad = from_behind(local_grad, "section", -1)
    weight_grad = lax.psum_scatter(
        lax.dot_general(
            prev_normed, grads_prev, (((0,), (0,)), ((), ())), preferred_element_type=jnp.float32
        ).astype(jnp.bfloat16),
        "fsdp",
        scatter_dimension=0,
        tiled=True,
    ).astype(jnp.float32)
    owned_gain = lax.dynamic_slice_in_dim(gain, lax.axis_index("fsdp") * owned, owned, 0)
    gain_part = jnp.sum(weight_rows.astype(jnp.float32) * weight_grad, axis=1) / owned_gain
    gain_grad = lax.all_gather(gain_part, "fsdp", axis=0, tiled=True)
    return (upstream_grad[None], weight_grad[None], gain_grad[None])


def solution(mesh):
    placed = (
        P("section", "fsdp", None),
        P("section", "fsdp", None),
        P("section", "fsdp", None),
        P("section", "fsdp", None),
        P("section", "fsdp", None),
        P("section", "fsdp", None),
        P("section", None),
    )
    return jax.shard_map(
        local,
        mesh=mesh,
        in_specs=placed,
        out_specs=(P("section", "fsdp", None), P("section", "fsdp", None), P("section", None)),
        check_vma=False,
    )
```

profile of v0, /device:TPU:0, one launch (start us, length us, event | category | flops | bytes accessed | tf_op | source)
XLA Modules:
  0.0 234.6 jit_solution(13687583729323604503)
XLA Ops:
  7.2 0.0 copy-start
  7.2 0.0 all-gather.4.cloned.1.call-start
  7.2 0.7 all-gather.4.cloned.1.call-update
  7.9 0.0 reduce-scatter.2.cloned.1.call-start
  8.0 2.2 fusion.2
  10.2 0.0 copy-done
  10.2 11.6 %convolution_convert_fusion = bf16[2048,3072]{1,0:T(8,128)(2,1)} fusion(bf16[1,512,3072]{2,1,0:T(8,128)(2,1)S(1)} %copy-done, bf16[1,512,2048]{2,1,0:T(8,128)(2,1)} %param.10, f32[2048]{0:T(1024)} %bitcast.39, f32[512]{0:T(512)S(1)} %add_rsqrt_fusion), kind=kOutput, calls=%fused_computation.2 | convolution fusion | flops 6452936704 | bytes 17836032 | tf_op jit(solution)/shard_map/dot_general | solution.py:48
  21.8 0.0 copy-start.3
  21.8 0.0 reduce-scatter.2.cloned.1.call-update
  21.8 81.0 %all-gather.4.cloned.1.call-done = bf16[1,2048,3072]{2,1,0:T(8,128)(2,1)} async-done(((bf16[1,128,3072]{2,1,0:T(8,128)(2,1)}), bf16[1,2048,3072]{2,1,0:T(8,128)(2,1)}) %all-gather.4.cloned.1.call-update) | async-done | bytes 12582928 | tf_op jit(solution)/shard_map/all_gather | solution.py:37
  102.8 0.0 copy-done.3
  102.8 0.0 copy-start.1
  102.8 0.0 copy-start.2
  102.9 11.3 %fusion.5 = (f32[512]{0:T(512)S(1)}, f32[512]{0:T(512)S(1)}, f32[512,2048]{1,0:T(8,128)S(1)}) fusion(bf16[1,512,2048]{2,1,0:T(8,128)(2,1)} %param.7, f32[2048]{0:T(1024)S(1)} %bitcast.40, bf16[1,2048,3072]{2,1,0:T(8,128)(2,1)} %all-gather.4.cloned.1.call-done, bf16[1,512,3072]{2,1,0:T(8,128)(2,1)} %param.9), kind=kOutput, calls=%fused_computation.11 | convolution fusion | flops 6448741376 | bytes 22032384 | tf_op jit(solution)/shard_map/dot_general | solution.py:21
  114.2 0.0 copy-done.1
  114.2 0.0 copy-done.2
  114.2 3.1 %fusion.10 = bf16[512,2048]{1,0:T(8,128)(2,1)} fusion(f32[512,2048]{1,0:T(8,128)S(1)} %get-tuple-element.5, bf16[1,512,2048]{2,1,0:T(8,128)(2,1)S(1)} %copy-done.2, bf16[1,512,2048]{2,1,0:T(8,128)(2,1)S(1)} %copy-done.1, f32[512]{0:T(512)S(1)} %get-tuple-element.7, f32[2048]{0:T(1024)S(1)} %bitcast.41, f32[512]{0:T(512)S(1)} %get-tuple-element.6), kind=kLoop, calls=%fused_computation.16 | loop fusion | flops 11534336 | bytes 10498048 | tf_op jit(solution)/shard_map/convert_element_type | solution.py:45
  117.3 1.3 collective-permute-start
  118.6 82.1 %reduce-scatter.2.cloned.1.call-done = bf16[128,3072]{1,0:T(8,128)(2,1)} async-done(((bf16[2048,3072]{1,0:T(8,128)(2,1)}), bf16[128,3072]{1,0:T(8,128)(2,1)}) %reduce-scatter.2.cloned.1.call-update) | async-done | bytes 786448 | tf_op jit(solution)/shard_map/reduce_scatter | solution.py:47
  200.6 1.7 fusion.18
  202.3 19.3 %all-gather.1 = f32[16,1,128]{2,1,0:T(1,128)S(1)} all-gather(f32[1,1,128]{2,1,0:T(1,128)S(1)} %fusion.19), channel_id=1, replica_groups=mesh['section'=8,'fsdp'=16] {'fsdp'}, dimensions={0}, use_global_device_ids=true | all-gather | bytes 8704 | tf_op jit(solution)/shard_map/all_gather | solution.py:57
  221.6 2.4 %convert_bitcast_fusion = f32[1,128,3072]{2,1,0:T(8,128)} fusion(bf16[128,3072]{1,0:T(8,128)(2,1)} %reduce-scatter.2.cloned.1.call-done), kind=kLoop, calls=%fused_computation.25 | loop fusion | flops 393216 | bytes 2359296 | tf_op jit(solution)/shard_map/broadcast_in_dim | solution.py:58
  224.0 0.0 collective-permute-done
  224.0 3.2 %copy.12 = bf16[1,512,2048]{2,1,0:T(8,128)(2,1)} copy(bf16[1,512,2048]{2,1,0:T(8,128)(2,1)} %bitcast.6) | data formatting | bytes 4194304
  227.2 0.6 copy.13
  (3 shorter events, 0.0 us)
Async XLA Ops:
  7.2 3.0 %copy-start = (bf16[1,512,3072]{2,1,0:T(8,128)(2,1)S(1)}, bf16[1,512,3072]{2,1,0:T(8,128)(2,1)}, u32[]{:S(2)}) copy-start(bf16[1,512,3072]{2,1,0:T(8,128)(2,1)} %param.11) | copy-start | bytes 9437188
  7.2 95.7 %all-gather.4.cloned.1.call-start = ((), (), s32[]{:S(2)}) async-start(), calls=%async_computation.2 | async-start | bytes 13369344 | tf_op jit(solution)/shard_map/all_gather | solution.py:37
  7.9 192.7 %reduce-scatter.2.cloned.1.call-start = ((), (), s32[]{:S(2)}) async-start(), calls=%async_computation.1 | async-start | bytes 13369344 | tf_op jit(solution)/shard_map/reduce_scatter | solution.py:47
  21.8 81.1 %copy-start.3 = (f32[1,2048]{1,0:T(1,128)S(1)}, f32[1,2048]{1,0:T(1,128)}, u32[]{:S(2)}) copy-start(f32[1,2048]{1,0:T(1,128)} %param.13) | copy-start | bytes 24580
  102.8 11.3 %copy-start.1 = (bf16[1,512,2048]{2,1,0:T(8,128)(2,1)S(1)}, bf16[1,512,2048]{2,1,0:T(8,128)(2,1)}, u32[]{:S(2)}) copy-start(bf16[1,512,2048]{2,1,0:T(8,128)(2,1)} %param.7) | copy-start | bytes 6291460
  102.8 11.3 %copy-start.2 = (bf16[1,512,2048]{2,1,0:T(8,128)(2,1)S(1)}, bf16[1,512,2048]{2,1,0:T(8,128)(2,1)}, u32[]{:S(2)}) copy-start(bf16[1,512,2048]{2,1,0:T(8,128)(2,1)} %param.8) | copy-start | bytes 6291460
  117.3 106.7 %collective-permute-start = (bf16[512,2048]{1,0:T(8,128)(2,1)}, bf16[512,2048]{1,0:T(8,128)(2,1)}, u32[]{:S(2)}, u32[]{:S(2)}) collective-permute-start(bf16[512,2048]{1,0:T(8,128)(2,1)} %fusion.10), channel_id=1, source_target_pairs={{16,0},{32,16},{48,32},{64,48},{80,64},{96,80},{112,96},{17,1},{33... | collective-permute-start | bytes 6291464 | tf_op jit(solution)/shard_map/ppermute | solution.py:12
Sparse Core Ops, SparseCore 0:
  10.2 92.5 all-gather.3
  106.3 94.3 reduce-scatter.1
where the time goes:
time: 235 us
  waiting for transfers between devices  164 us (70%)
  matrix products  22.9 us (10%)
  blocking collectives  19.3 us (8%)
  between operations  14.1 us (6%)
  other arithmetic  9.45 us (4%)
  local copies, waits for them, and re-layouts  3.78 us (2%)
    reduce_scatter x1, waiting for transfers between devices, local(): lax.psum_scatter(lax.dot_general(prev_normed, grads_prev, (((0,), (0,)),...  82.1 us
    all_gather x1, waiting for transfers between devices, local(): lax.all_gather(weight_rows, 'fsdp', axis=0, tiled=True)  81 us
    all_gather x1, blocking collectives, local(): gain_grad = lax.all_gather(gain_part, 'fsdp', axis=0, tiled=True)  19.3 us
    dot_general x1, matrix products, local(): lax.dot_general(prev_normed, grads_prev, (((0,), (0,)), ((), ())), prefer...  11.6 us
    dot_general x1, matrix products, transpose_product(): lax.dot_general(grads, piece, (((1,), (1,)), ((), ())), preferred_element...  11.3 us
  transfers between devices with their start and end apart: 3, of which 2 were waited for; matrix products, arithmetic and copies ran while one was open for 14% of the time, Pallas kernels for 0%

commit v1 on v0

--- a/solution.py
+++ b/solution.py
@@ -34,7 +34,10 @@
     prev_scale = row_scale(rows_prev)
     prev_normed = (rows_prev.astype(jnp.float32) * prev_scale * gain[None, :]).astype(jnp.bfloat16)
     direction = transpose_product(
-        grads_now, lax.all_gather(weight_rows, "fsdp", axis=0, tiled=True)
+        grads_now,
+        jnp.concatenate(
+            lax.all_to_all(jnp.stack([weight_rows] * lax.axis_size("fsdp")), "fsdp", 0, 0), axis=0
+        ),
     )
     scale = row_scale(rows_now)
     values = rows_now.astype(jnp.float32)

time: 235 us -> 288 us (1.23); the launches traced: 235 us -> 284 us
  blocking collectives: 19.3 us -> 204 us
  waiting for transfers between devices: 164 us -> 21.2 us
  local copies, waits for them, and re-layouts: 3.78 us -> 11.2 us
    all_to_all x0 -> x1, blocking collectives: none -> 184 us  [local(): lax.all_to_all(jnp.stack([weight_rows] * lax.axis_size('fsdp')), 'fsdp',...]
    all_gather x1 -> x0, waiting for transfers between devices: 81 us -> none  [local(): lax.all_gather(weight_rows, 'fsdp', axis=0, tiled=True)]
    reduce_scatter x1, waiting for transfers between devices: 82.1 us -> 16.1 us  [local(): lax.psum_scatter(lax.dot_general(prev_normed, grads_prev, (((0,), (0,)),...]
    another operation x0 -> x1, local copies, waits for them, and re-layouts: none -> 7.2 us  [local(): jnp.stack([weight_rows] * lax.axis_size('fsdp'))]
    ppermute x1, waiting for transfers between devices: 0.01 us -> 5.09 us  [from_behind(): return lax.ppermute(block, axis, route)]
  transfers between devices with their start and end apart: 3 -> 2, of which waited for: 2 -> 2; matrix products, arithmetic and copies ran while one was open for 14% -> 8% of each run, Pallas kernels for 0% -> 0%
where the time goes in v1:
time: 288 us; the launch traced here: 284 us
  blocking collectives  204 us (71%)
  waiting for transfers between devices  21.2 us (7%)
  matrix products  20.6 us (7%)
  between operations  14.1 us (5%)
  other arithmetic  11.8 us (4%)
  local copies, waits for them, and re-layouts  11.2 us (4%)
    all_to_all x1, blocking collectives, local(): lax.all_to_all(jnp.stack([weight_rows] * lax.axis_size('fsdp')), 'fsdp',...  184 us
    all_gather x1, blocking collectives, local(): gain_grad = lax.all_gather(gain_part, 'fsdp', axis=0, tiled=True)  19.4 us
    reduce_scatter x1, waiting for transfers between devices, local(): lax.psum_scatter(lax.dot_general(prev_normed, grads_prev, (((0,), (0,)),...  16.1 us
    dot_general x1, matrix products, local(): lax.dot_general(prev_normed, grads_prev, (((0,), (0,)), ((), ())), prefer...  11.6 us
    dot_general x1, matrix products, transpose_product(): lax.dot_general(grads, piece, (((1,), (1,)), ((), ())), preferred_element...  9.05 us
    another operation x1, local copies, waits for them, and re-layouts, local(): jnp.stack([weight_rows] * lax.axis_size('fsdp'))  7.2 us
  transfers between devices with their start and end apart: 2, of which 2 were waited for; matrix products, arithmetic and copies ran while one was open for 8% of the time, Pallas kernels for 0%

profile of v1, /device:TPU:0, one launch (start us, length us, event | category | flops | bytes accessed | tf_op | source)
XLA Modules:
  0.0 283.8 jit_solution(3455203910167941436)
XLA Ops:
  7.2 0.0 copy-start
  7.2 0.0 reduce-scatter.2.cloned.1.call-start
  7.2 2.2 fusion
  9.5 0.2 copy-done
  9.7 11.6 %convolution_convert_fusion = bf16[2048,3072]{1,0:T(8,128)(2,1)} fusion(bf16[1,512,3072]{2,1,0:T(8,128)(2,1)S(1)} %copy-done, bf16[1,512,2048]{2,1,0:T(8,128)(2,1)} %param.10, f32[2048]{0:T(1024)} %bitcast.37, f32[512]{0:T(512)S(1)} %add_rsqrt_fusion), kind=kOutput, calls=%fused_computation | convolution fusion | flops 6452936704 | bytes 17836032 | tf_op jit(solution)/shard_map/dot_general | solution.py:51
  21.3 0.0 reduce-scatter.2.cloned.1.call-update
  21.3 7.2 %stack.3 = bf16[16,128,3072]{2,1,0:T(8,128)(2,1)} broadcast(bf16[128,3072]{1,0:T(8,128)(2,1)} %bitcast.35), dimensions={1,2} | broadcast | bytes 13369344 | tf_op jit(solution)/shard_map/stack | solution.py:39
  28.5 0.0 copy-start.1
  28.5 184.2 %all_to_all.5 = bf16[16,128,3072]{2,1,0:T(8,128)(2,1)S(1)} all-to-all(bf16[16,128,3072]{2,1,0:T(8,128)(2,1)} %stack.3), channel_id=1, replica_groups=mesh['section'=8,'fsdp'=16] {'fsdp'}, dimensions={0} | all-to-all | bytes 25165824 | tf_op jit(solution)/shard_map/all_to_all | solution.py:39
  212.7 0.0 copy-done.1
  212.7 9.1 %fusion.3 = (f32[512]{0:T(512)S(1)}, f32[512]{0:T(512)S(1)}, f32[512,2048]{1,0:T(8,128)S(1)}) fusion(bf16[1,512,2048]{2,1,0:T(8,128)(2,1)} %param.7, f32[2048]{0:T(1024)S(1)} %bitcast.38, bf16[2048,3072]{1,0:T(8,128)(2,1)S(1)} %bitcast.34, bf16[1,512,3072]{2,1,0:T(8,128)(2,1)} %param.9), kind=kOutput, calls=%fused_computation.9 | convolution fusion | flops 6448741376 | bytes 22032384 | tf_op jit(solution)/shard_map/dot_general | solution.py:21
  221.8 5.4 %fusion.8 = bf16[512,2048]{1,0:T(8,128)(2,1)} fusion(f32[512,2048]{1,0:T(8,128)S(1)} %get-tuple-element.5, bf16[1,512,2048]{2,1,0:T(8,128)(2,1)} %param.8, bf16[1,512,2048]{2,1,0:T(8,128)(2,1)} %param.7, f32[512]{0:T(512)S(1)} %get-tuple-element.7, f32[2048]{0:T(1024)S(1)} %bitcast.39, f32[512]{0:T(512)S(1)} %get-tuple-element.6), kind=kLoop, calls=%fused_computation.14 | loop fusion | flops 11534336 | bytes 10498048 | tf_op jit(solution)/shard_map/convert_element_type | solution.py:48
  227.2 1.3 collective-permute-start
  228.5 5.1 %collective-permute-done = bf16[512,2048]{1,0:T(8,128)(2,1)} collective-permute-done((bf16[512,2048]{1,0:T(8,128)(2,1)}, bf16[512,2048]{1,0:T(8,128)(2,1)}, u32[]{:S(2)}, u32[]{:S(2)}) %collective-permute-start) | collective-permute-done | bytes 2097184 | tf_op jit(solution)/shard_map/ppermute | solution.py:12
  233.6 16.1 %reduce-scatter.2.cloned.1.call-done = bf16[128,3072]{1,0:T(8,128)(2,1)} async-done(((bf16[2048,3072]{1,0:T(8,128)(2,1)}), bf16[128,3072]{1,0:T(8,128)(2,1)}) %reduce-scatter.2.cloned.1.call-update) | async-done | bytes 786448 | tf_op jit(solution)/shard_map/reduce_scatter | solution.py:50
  249.7 1.7 fusion.17
  251.4 19.4 %all-gather = f32[16,1,128]{2,1,0:T(1,128)S(1)} all-gather(f32[1,1,128]{2,1,0:T(1,128)S(1)} %fusion.18), channel_id=1, replica_groups=mesh['section'=8,'fsdp'=16] {'fsdp'}, dimensions={0}, use_global_device_ids=true | all-gather | bytes 8704 | tf_op jit(solution)/shard_map/all_gather | solution.py:60
  270.8 2.4 convert_bitcast_fusion
  273.2 3.2 %copy.12 = bf16[1,512,2048]{2,1,0:T(8,128)(2,1)} copy(bf16[1,512,2048]{2,1,0:T(8,128)(2,1)} %bitcast.7) | data formatting | bytes 4194304
  276.4 0.6 copy.13
  (3 shorter events, 0.0 us)
Async XLA Ops:
  7.2 2.5 copy-start
  7.2 242.6 %reduce-scatter.2.cloned.1.call-start = ((), (), s32[]{:S(2)}) async-start(), calls=%async_computation.2 | async-start | bytes 13369344 | tf_op jit(solution)/shard_map/reduce_scatter | solution.py:50
  28.5 184.2 %copy-start.1 = (f32[1,2048]{1,0:T(1,128)S(1)}, f32[1,2048]{1,0:T(1,128)}, u32[]{:S(2)}) copy-start(f32[1,2048]{1,0:T(1,128)} %param.13) | copy-start | bytes 24580
  227.2 6.4 %collective-permute-start = (bf16[512,2048]{1,0:T(8,128)(2,1)}, bf16[512,2048]{1,0:T(8,128)(2,1)}, u32[]{:S(2)}, u32[]{:S(2)}) collective-permute-start(bf16[512,2048]{1,0:T(8,128)(2,1)} %fusion.8), channel_id=1, source_target_pairs={{16,0},{32,16},{48,32},{64,48},{80,64},{96,80},{112,96},{17,1},{33... | collective-permute-start | bytes 6291464 | tf_op jit(solution)/shard_map/ppermute | solution.py:12
Sparse Core Ops, SparseCore 0:
  21.4 228.2 reduce-scatter.1
